TPU v7x, 32 devices: a whole 2x2x4 slice. The times are simulated.
32 devices in a mesh: expert: 16 (over z, y, x), replica: 2 (over core).
Axes of the slice: x: 2, y: 2, z: 4, core: 2. Of those that a mesh axis runs over, the one named last changes fastest.
Arguments:
- tokens: bfloat16 [1024, 7168], P('expert', 'replica'), may hold values from -6 to 6
- routes: int32 [1024, 8], P('expert'), may hold values from 0 to 15, all different within a row; in each aligned block of 64 rows (0 to 63, 64 to 127, ...) at most 64 rows name the same one
- route_scores: float32 [1024, 8], P('expert'), may hold values from 0.05 to 1
- placement: int32 [16], replicated, may hold values from 0 to 15, each once
- w_in: bfloat16 [16, 7168, 2, 1024], P('expert', 'replica'), may hold values from -0.0625 to 0.0625
- w_out: bfloat16 [16, 1024, 7168], P('expert', None, 'replica'), may hold values from -0.1875 to 0.1875
Outputs:
- mixed: bfloat16 [1024, 7168], P('expert', 'replica')
Inputs may be any that keep to these rules, and one draw needn't show every extreme that they name: `routes`: each row names 8 different logical experts. Among the 64 rows of each aligned block (the tokens of one index of the expert axis) no expert is named by more than 64 rows, a bound that some block reaches. `placement`: A permutation of the physical slots.
All inputs are finite; a program needn't handle non-finite values.
Results may differ from a plain program's by a relative error of at most 0.0057.
Values may be sent and summed in bfloat16 or wider, within the bound.
A program may use at most 128 MiB of HBM per device.

v0:
```python
import jax
import jax.numpy as jnp
from jax import lax
from jax.sharding import PartitionSpec as P


def on_device(tokens, routes, route_scores, placement, w_in, w_out):
    tok_rows, feature_cols = tokens.shape
    route_count = routes.shape[1]
    experts = placement.shape[0]
    hidden_units = w_in.shape[3]
    capacity = min(tok_rows, max(2, 2 * tok_rows * route_count // experts))
    slot_total = experts * capacity
    expert_ids = jnp.arange(experts, dtype=jnp.int32)
    route_table = routes[:, :, None] == expert_ids
    physical = jnp.sum(jnp.where(route_table, placement, 0), axis=-1)
    flat_slots = physical.reshape(-1)
    onehot = (flat_slots[:, None] == expert_ids).astype(jnp.int32)
    earlier = jnp.sum((jnp.cumsum(onehot, axis=0) - onehot) * onehot, axis=1)
    position = (flat_slots * capacity + earlier).reshape(tok_rows, route_count)
    slot_index = jnp.arange(slot_total, dtype=jnp.int32)
    placing = jnp.any(position[None, :, :] == slot_index[:, None, None], axis=-1).astype(
        jnp.bfloat16
    )
    outgoing = jnp.dot(placing, tokens, preferred_element_type=jnp.float32).astype(jnp.bfloat16)
    incoming = lax.all_to_all(outgoing, "expert", split_axis=0, concat_axis=0, tiled=True)
    weights_in = w_in[0].reshape(feature_cols, 2 * hidden_units)
    weights_out = w_out[0]
    partial_value = jnp.dot(incoming, weights_in, preferred_element_type=jnp.float32)
    partial_value = partial_value.reshape(slot_total, 2, hidden_units)
    shares = lax.psum_scatter(partial_value, "replica", scatter_dimension=2, tiled=True)
    active = (jax.nn.silu(shares[:, 0]) * shares[:, 1]).astype(jnp.bfloat16)
    result = jnp.dot(
        lax.all_gather(active, "replica", axis=1, tiled=True),
        weights_out,
        preferred_element_type=jnp.float32,
    )
    expert_out = result.astype(jnp.bfloat16)
    returned = lax.all_to_all(expert_out, "expert", split_axis=0, concat_axis=0, tiled=True)
    route_weight = 2.5 * route_scores / jnp.sum(route_scores, axis=1, keepdims=True)
    picked = returned[position.reshape(-1)].reshape(tok_rows, route_count, feature_cols)
    mixed = jnp.sum(picked.astype(jnp.float32) * route_weight[:, :, None], axis=1)
    return mixed.astype(jnp.bfloat16)


def solution(mesh):
    in_specs = (
        P("expert", "replica"),
        P("expert", None),
        P("expert", None),
        P(),
        P("expert", "replica", None, None),
        P("expert", None, "replica"),
    )
    out_specs = P("expert", "replica")
    return jax.shard_map(
        on_device, mesh=mesh, in_specs=in_specs, out_specs=out_specs, check_vma=False
    )
```

profile of v0, /device:TPU:28, one launch (start us, length us, event | category | flops | bytes accessed | tf_op | source)
XLA Modules:
  0.0 454.1 jit_solution(2317390866444530714)
XLA Ops:
  6.5 0.8 select_reduce_fusion
  7.5 0.1 eq.58
  7.6 0.1 eq.54
  7.7 1.2 reduce-window.6
  8.8 0.2 slice_reduce_fusion
  9.1 0.1 fusion.7
  9.2 0.1 reduce_sum.42
  9.3 0.1 copy.18
  9.4 0.7 fusion.4
  10.2 5.1 %convolution_convert_fusion.1 = bf16[1024,3584]{1,0:T(8,128)(2,1)} fusion(pred[1024,64]{0,1:T(8,128)(4,1)S(1)} %fusion.4, bf16[64,3584]{1,0:T(8,128)(2,1)S(1)} %copy-done), kind=kOutput, calls=%fused_computation.2 | convolution fusion | flops 473432064 | bytes 7864320 | tf_op jit(solution)/shard_map/dot_general | solution.py:25
  15.3 7.0 %all-to-all-start = ((bf16[16,64,3584]{2,1,0:T(8,128)(2,1)}), bf16[16,64,3584]{2,1,0:T(8,128)(2,1)}, u32[]{:S(2)}, u32[]{:S(2)}) async-start(bf16[16,64,3584]{2,1,0:T(8,128)(2,1)} %bitcast.55), calls=%async_computation | async-start | bytes 14680064 | tf_op jit(solution)/shard_map/all_to_all | solution.py:26
  22.3 16.0 %copy.23 = bf16[448,8,2,1024]{3,1,2,0:T(8,128)(2,1)} copy(bf16[448,8,2,1024]{3,2,1,0:T(2,128)(2,1)} %bitcast.56) | data formatting | bytes 29360128
  38.3 18.8 %copy.19 = bf16[2048,3584]{1,0:T(8,128)(2,1)} copy(bf16[2048,3584]{0,1:T(8,128)(2,1)} %bitcast.54) | data formatting | bytes 29360128 | tf_op jit(solution)/shard_map/dot_general | solution.py:29
  57.1 131.5 %all-to-all-done = bf16[16,64,3584]{2,1,0:T(8,128)(2,1)} async-done(((bf16[16,64,3584]{2,1,0:T(8,128)(2,1)}), bf16[16,64,3584]{2,1,0:T(8,128)(2,1)}, u32[]{:S(2)}, u32[]{:S(2)}) %all-to-all-start) | async-done | bytes 7340064 | tf_op jit(solution)/shard_map/all_to_all | solution.py:26
  188.6 21.6 %fusion.10 = f32[1024,2,1024]{2,0,1:T(8,128)} fusion(bf16[1024,3584,1]{1,0,2:T(8,128)(2,1)} %bitcast.3, bf16[2,1024,3584]{2,1,0:T(8,128)(2,1)} %bitcast.57), kind=kOutput, calls=%fused_computation.28 | convolution fusion | flops 15032385536 | bytes 30408704 | tf_op jit(solution)/shard_map/dot_general | solution.py:29
  210.2 16.7 %reduce-scatter.2.cloned.1.call-done = f32[1024,2,512]{2,0,1:T(8,128)} async-done(((f32[1024,2,1024]{2,0,1:T(8,128)}), f32[1024,2,512]{2,0,1:T(8,128)}) %reduce-scatter.2.cloned.1.call-update) | async-done | bytes 4194320 | tf_op jit(solution)/shard_map/reduce_scatter | solution.py:31
  226.9 3.8 fusion.3
  230.8 11.9 %all-gather.2.cloned.1.call-done = bf16[1024,1024]{1,0:T(8,128)(2,1)} async-done(((bf16[1024,512]{1,0:T(8,128)(2,1)}), bf16[1024,1024]{1,0:T(8,128)(2,1)}) %all-gather.2.cloned.1.call-update) | async-done | bytes 2097168 | tf_op jit(solution)/shard_map/all_gather | solution.py:34
  242.7 12.5 %convolution_convert_fusion = bf16[1024,3584]{1,0:T(8,128)(2,1)} fusion(bf16[1024,1024]{1,0:T(8,128)(2,1)} %all-gather.2.cloned.1.call-done, bf16[1,1024,3584]{2,1,0:T(8,128)(2,1)} %param.11), kind=kOutput, calls=%fused_computation.1 | convolution fusion | flops 7519862784 | bytes 16777216 | tf_op jit(solution)/shard_map/dot_general | solution.py:33
  255.2 7.1 %all-to-all-start.1 = ((bf16[16,64,3584]{2,1,0:T(8,128)(2,1)}), bf16[16,64,3584]{2,1,0:T(8,128)(2,1)}, u32[]{:S(2)}, u32[]{:S(2)}) async-start(bf16[16,64,3584]{2,1,0:T(8,128)(2,1)} %bitcast.58), calls=%async_computation.2 | async-start | bytes 14680064 | tf_op jit(solution)/shard_map/all_to_all | solution.py:39
  262.4 0.1 mul.49
  262.6 166.8 %all-to-all-done.1 = bf16[16,64,3584]{2,1,0:T(8,128)(2,1)} async-done(((bf16[16,64,3584]{2,1,0:T(8,128)(2,1)}), bf16[16,64,3584]{2,1,0:T(8,128)(2,1)}, u32[]{:S(2)}, u32[]{:S(2)}) %all-to-all-start.1) | async-done | bytes 7340064 | tf_op jit(solution)/shard_map/all_to_all | solution.py:39
  429.4 12.0 %gather_fusion = bf16[512,3584]{1,0:T(8,128)(2,1)} fusion(bf16[1024,3584]{1,0:T(8,128)(2,1)} %bitcast.10, s32[1024]{0:T(1024)S(1)} %pad_clamp_fusion), kind=kCustom, calls=%fused_computation | custom fusion | bytes 7342080 | tf_op jit(solution)/shard_map/gather | solution.py:41
  441.4 5.8 %fusion = bf16[64,3584]{1,0:T(8,128)(2,1)} fusion(bf16[512,3584]{1,0:T(8,128)(2,1)} %gather_fusion, f32[64,8]{1,0:T(8,128)S(1)} %copy.21), kind=kLoop, calls=%fused_computation.4 | loop fusion | flops 5275648 | bytes 4130816 | tf_op jit(solution)/shard_map/reduce_sum | solution.py:42
  (22 shorter events, 0.5 us)
Async XLA Ops:
  6.5 3.6 copy-start
  15.3 173.3 %all-to-all-start = ((bf16[16,64,3584]{2,1,0:T(8,128)(2,1)}), bf16[16,64,3584]{2,1,0:T(8,128)(2,1)}, u32[]{:S(2)}, u32[]{:S(2)}) async-start(bf16[16,64,3584]{2,1,0:T(8,128)(2,1)} %bitcast.55), calls=%async_computation | async-start | bytes 14680064 | tf_op jit(solution)/shard_map/all_to_all | solution.py:26
  22.2 204.7 %reduce-scatter.2.cloned.1.call-start = ((), (), s32[]{:S(2)}) async-start(), calls=%async_computation.3 | async-start | bytes 12582912 | tf_op jit(solution)/shard_map/reduce_scatter | solution.py:31
  210.2 32.5 %all-gather.2.cloned.1.call-start = ((), (), s32[]{:S(2)}) async-start(), calls=%async_computation.4 | async-start | bytes 3145728 | tf_op jit(solution)/shard_map/all_gather | solution.py:34
  255.2 7.2 %copy-start.2 = (f32[64,8]{0,1:T(8,128)S(1)}, f32[64,8]{0,1:T(8,128)}, u32[]{:S(2)}) copy-start(f32[64,8]{0,1:T(8,128)} %param.8) | copy-start | bytes 6148
  255.2 174.2 %all-to-all-start.1 = ((bf16[16,64,3584]{2,1,0:T(8,128)(2,1)}), bf16[16,64,3584]{2,1,0:T(8,128)(2,1)}, u32[]{:S(2)}, u32[]{:S(2)}) async-start(bf16[16,64,3584]{2,1,0:T(8,128)(2,1)} %bitcast.58), calls=%async_computation.2 | async-start | bytes 14680064 | tf_op jit(solution)/shard_map/all_to_all | solution.py:39
  429.4 17.8 %copy-start.1 = (bf16[64,3584]{1,0:T(8,128)(2,1)S(1)}, bf16[64,3584]{1,0:T(8,128)(2,1)}, u32[]{:S(2)}) copy-start(bf16[64,3584]{1,0:T(8,128)(2,1)} %param.6) | copy-start | bytes 1376260
Sparse Core Ops, SparseCore 0:
  210.3 16.5 reduce-scatter.1
  230.9 11.7 all-gather.1
where the time goes:
time: 455 us; the launch traced here: 454 us
  waiting for transfers between devices  327 us (72%)
  local copies, waits for them, and re-layouts  47.8 us (11%)
  matrix products  39.3 us (9%)
  starting transfers between devices  14.1 us (3%)
  between operations  13.5 us (3%)
  other arithmetic  12.6 us (3%)
    all_to_all x1, waiting for transfers between devices, on_device(): lax.all_to_all(expert_out, 'expert', split_axis=0, concat_axis=0, tiled=T...  167 us
    all_to_all x1, waiting for transfers between devices, on_device(): lax.all_to_all(outgoing, 'expert', split_axis=0, concat_axis=0, tiled=True)  131 us
    dot_general x1, matrix products, on_device(): jnp.dot(incoming, weights_in, preferred_element_type=jnp.float32)  21.6 us
    dot_general x1, local copies, waits for them, and re-layouts, on_device(): jnp.dot(incoming, weights_in, preferred_element_type=jnp.float32)  18.8 us
    reduce_scatter x1, waiting for transfers between devices, on_device(): lax.psum_scatter(partial_value, 'replica', scatter_dimension=2, tiled=True)  16.7 us
    unnamed x7, local copies, waits for them, and re-layouts  16 us
    dot_general x1, matrix products, on_device(): jnp.dot(lax.all_gather(active, 'replica', axis=1, tiled=True), weights_ou...  12.5 us
    gather x1, local copies, waits for them, and re-layouts, on_device(): returned[position.reshape(-1)].reshape(tok_rows, route_count, feature_cols)  12 us
  transfers between devices with their start and end apart: 4, of which 4 were waited for; matrix products, arithmetic and copies ran while one was open for 8% of the time, Pallas kernels for 0%

commit v1 on v0

--- a/solution.py
+++ b/solution.py
@@ -2,6 +2,7 @@
 import jax.numpy as jnp
 from jax import lax
 from jax.sharding import PartitionSpec as P
+from jax.lax import axis_index, ppermute, psum
 
 
 def on_device(tokens, routes, route_scores, placement, w_in, w_out):
@@ -36,7 +37,17 @@
         preferred_element_type=jnp.float32,
     )
     expert_out = result.astype(jnp.bfloat16)
-    returned = lax.all_to_all(expert_out, "expert", split_axis=0, concat_axis=0, tiled=True)
+    e_now, w2 = (psum(1, "expert"), axis_index("expert"))
+    piece_next = expert_out.shape[0] // e_now
+    work_now = jnp.roll(expert_out, -w2 * piece_next, axis=0)
+    nodes = [lax.slice_in_dim(work_now, 0, piece_next, axis=0)]
+    for dev in range(1, e_now):
+        extra = lax.slice_in_dim(work_now, dev * piece_next, (dev + 1) * piece_next, axis=0)
+        nodes.append(
+            ppermute(extra, "expert", [(num, (num + dev) % e_now) for num in range(e_now)])
+        )
+    s_next = jnp.concatenate(nodes[::-1], axis=0)
+    returned = jnp.roll(s_next, (w2 + 1) * nodes[0].shape[0], axis=0)
     route_weight = 2.5 * route_scores / jnp.sum(route_scores, axis=1, keepdims=True)
     picked = returned[position.reshape(-1)].reshape(tok_rows, route_count, feature_cols)
     mixed = jnp.sum(picked.astype(jnp.float32) * route_weight[:, :, None], axis=1)

time: 455 us -> 526 us (1.16)
  the two profiles are of different devices: /device:TPU:28 before, /device:TPU:8 now
where the time goes in v1:
time: 526 us; the launch traced here: 525 us
  waiting for transfers between devices  302 us (57%)
  local copies, waits for them, and re-layouts  67.1 us (13%)
  starting transfers between devices  65.5 us (12%)
  matrix products  39.2 us (7%)
  other arithmetic  37.6 us (7%)
  between operations  13.5 us (3%)
    ppermute x15, waiting for transfers between devices, on_device(): ppermute(extra, 'expert', [(num, (num + dev) % e_now) for num in range(e_...  143 us
    all_to_all x1, waiting for transfers between devices, on_device(): lax.all_to_all(outgoing, 'expert', split_axis=0, concat_axis=0, tiled=True)  123 us
    ppermute x15, starting transfers between devices, on_device(): ppermute(extra, 'expert', [(num, (num + dev) % e_now) for num in range(e_...  58 us
    unnamed x22, local copies, waits for them, and re-layouts  28.2 us
    reduce_scatter x1, waiting for transfers between devices, on_device(): lax.psum_scatter(partial_value, 'replica', scatter_dimension=2, tiled=True)  24.6 us
    dot_general x1, matrix products, on_device(): jnp.dot(incoming, weights_in, preferred_element_type=jnp.float32)  21.6 us
    dot_general x1, local copies, waits for them, and re-layouts, on_device(): jnp.dot(incoming, weights_in, preferred_element_type=jnp.float32)  18.7 us
    concatenate x1, other arithmetic, on_device(): work_now = jnp.roll(expert_out, -w2 * piece_next, axis=0)  12.5 us
  transfers between devices with their start and end apart: 18, of which 15 were waited for; matrix products, arithmetic and copies ran while one was open for 9% of the time, Pallas kernels for 0%

profile of v1, /device:TPU:8, one launch (start us, length us, event | category | flops | bytes accessed | tf_op | source)
XLA Modules:
  0.0 525.2 jit_solution(9416930360163315893)
XLA Ops:
  10.2 5.1 convolution_convert_fusion.1
  15.3 7.2 %all-to-all-start = ((bf16[16,64,3584]{2,1,0:T(8,128)(2,1)}), bf16[16,64,3584]{2,1,0:T(8,128)(2,1)}, u32[]{:S(2)}, u32[]{:S(2)}) async-start(bf16[16,64,3584]{2,1,0:T(8,128)(2,1)} %bitcast.53), calls=%async_computation | async-start | bytes 14680064 | tf_op jit(solution)/shard_map/all_to_all | solution.py:27
  22.5 16.0 %copy.23 = bf16[448,8,2,1024]{3,1,2,0:T(8,128)(2,1)} copy(bf16[448,8,2,1024]{3,2,1,0:T(2,128)(2,1)} %bitcast.54) | data formatting | bytes 29360128
  38.6 18.7 %copy.19 = bf16[2048,3584]{1,0:T(8,128)(2,1)} copy(bf16[2048,3584]{0,1:T(8,128)(2,1)} %bitcast.52) | data formatting | bytes 29360128 | tf_op jit(solution)/shard_map/dot_general | solution.py:30
  57.3 123.4 %all-to-all-done = bf16[16,64,3584]{2,1,0:T(8,128)(2,1)} async-done(((bf16[16,64,3584]{2,1,0:T(8,128)(2,1)}), bf16[16,64,3584]{2,1,0:T(8,128)(2,1)}, u32[]{:S(2)}, u32[]{:S(2)}) %all-to-all-start) | async-done | bytes 7340064 | tf_op jit(solution)/shard_map/all_to_all | solution.py:27
  180.8 21.6 %fusion.13 = f32[1024,2,1024]{2,0,1:T(8,128)} fusion(bf16[1024,3584,1]{1,0,2:T(8,128)(2,1)} %bitcast.3, bf16[2,1024,3584]{2,1,0:T(8,128)(2,1)} %bitcast.55), kind=kOutput, calls=%fused_computation.51 | convolution fusion | flops 15032385536 | bytes 30408704 | tf_op jit(solution)/shard_map/dot_general | solution.py:30
  202.6 24.6 %reduce-scatter.2.cloned.1.call-done = f32[1024,2,512]{2,0,1:T(8,128)} async-done(((f32[1024,2,1024]{2,0,1:T(8,128)}), f32[1024,2,512]{2,0,1:T(8,128)}) %reduce-scatter.2.cloned.1.call-update) | async-done | bytes 4194320 | tf_op jit(solution)/shard_map/reduce_scatter | solution.py:32
  231.3 11.7 %all-gather.2.cloned.1.call-done = bf16[1024,1024]{1,0:T(8,128)(2,1)} async-done(((bf16[1024,512]{1,0:T(8,128)(2,1)}), bf16[1024,1024]{1,0:T(8,128)(2,1)}) %all-gather.2.cloned.1.call-update) | async-done | bytes 2097168 | tf_op jit(solution)/shard_map/all_gather | solution.py:35
  242.9 12.5 %convolution_convert_fusion = bf16[1024,3584]{1,0:T(8,128)(2,1)} fusion(bf16[1024,1024]{1,0:T(8,128)(2,1)} %all-gather.2.cloned.1.call-done, bf16[1,1024,3584]{2,1,0:T(8,128)(2,1)} %param.13), kind=kOutput, calls=%fused_computation.5 | convolution fusion | flops 7519862784 | bytes 16777216 | tf_op jit(solution)/shard_map/dot_general | solution.py:34
  255.4 12.5 %fusion.1 = bf16[1024,3584]{1,0:T(8,128)(2,1)} fusion(s32[]{:T(128)S(6)} %select_n.29, bf16[1024,3584]{1,0:T(8,128)(2,1)} %convolution_convert_fusion), kind=kLoop, calls=%fused_computation.8 | loop fusion | flops 14680064 | bytes 14680068 | tf_op jit(solution)/shard_map/jit(_roll_dynamic)/concatenate | solution.py:42
  281.5 11.0 %collective-permute-done = bf16[64,3584]{1,0:T(8,128)(2,1)S(1)} collective-permute-done((bf16[64,3584]{1,0:T(8,128)(2,1)}, bf16[64,3584]{1,0:T(8,128)(2,1)S(1)}, u32[]{:S(2)}, u32[]{:S(2)}) %collective-permute-start) | collective-permute-done | bytes 458784 | tf_op jit(solution)/shard_map/ppermute | solution.py:47
  292.5 5.8 %collective-permute-start.5 = (bf16[64,3584]{1,0:T(8,128)(2,1)}, bf16[64,3584]{1,0:T(8,128)(2,1)S(1)}, u32[]{:S(2)}, u32[]{:S(2)}) collective-permute-start(bf16[64,3584]{1,0:T(8,128)(2,1)} %get-tuple-element.15), channel_id=1, source_target_pairs={{0,20},{2,22},{4,24},{6,26},{8,28},{10,30},{12,0},{14,2},{16,4},{1... | collective-permute-start | bytes 1376264 | tf_op jit(solution)/shard_map/ppermute | solution.py:47
  299.1 9.3 %collective-permute-done.1 = bf16[64,3584]{1,0:T(8,128)(2,1)S(1)} collective-permute-done((bf16[64,3584]{1,0:T(8,128)(2,1)}, bf16[64,3584]{1,0:T(8,128)(2,1)S(1)}, u32[]{:S(2)}, u32[]{:S(2)}) %collective-permute-start.1) | collective-permute-done | bytes 458784 | tf_op jit(solution)/shard_map/ppermute | solution.py:47
  309.1 9.0 %collective-permute-done.2 = bf16[64,3584]{1,0:T(8,128)(2,1)S(1)} collective-permute-done((bf16[64,3584]{1,0:T(8,128)(2,1)}, bf16[64,3584]{1,0:T(8,128)(2,1)S(1)}, u32[]{:S(2)}, u32[]{:S(2)}) %collective-permute-start.2) | collective-permute-done | bytes 458784 | tf_op jit(solution)/shard_map/ppermute | solution.py:47
  321.3 8.8 %collective-permute-done.3 = bf16[64,3584]{1,0:T(8,128)(2,1)S(1)} collective-permute-done((bf16[64,3584]{1,0:T(8,128)(2,1)}, bf16[64,3584]{1,0:T(8,128)(2,1)S(1)}, u32[]{:S(2)}, u32[]{:S(2)}) %collective-permute-start.3) | collective-permute-done | bytes 458784 | tf_op jit(solution)/shard_map/ppermute | solution.py:47
  331.0 27.9 %collective-permute-done.4 = bf16[64,3584]{1,0:T(8,128)(2,1)S(1)} collective-permute-done((bf16[64,3584]{1,0:T(8,128)(2,1)}, bf16[64,3584]{1,0:T(8,128)(2,1)S(1)}, u32[]{:S(2)}, u32[]{:S(2)}) %collective-permute-start.4) | collective-permute-done | bytes 458784 | tf_op jit(solution)/shard_map/ppermute | solution.py:47
  359.8 35.1 %collective-permute-done.5 = bf16[64,3584]{1,0:T(8,128)(2,1)S(1)} collective-permute-done((bf16[64,3584]{1,0:T(8,128)(2,1)}, bf16[64,3584]{1,0:T(8,128)(2,1)S(1)}, u32[]{:S(2)}, u32[]{:S(2)}) %collective-permute-start.5) | collective-permute-done | bytes 458784 | tf_op jit(solution)/shard_map/ppermute | solution.py:47
  395.7 9.9 %collective-permute-done.6 = bf16[64,3584]{1,0:T(8,128)(2,1)S(1)} collective-permute-done((bf16[64,3584]{1,0:T(8,128)(2,1)}, bf16[64,3584]{1,0:T(8,128)(2,1)S(1)}, u32[]{:S(2)}, u32[]{:S(2)}) %collective-permute-start.6) | collective-permute-done | bytes 458784 | tf_op jit(solution)/shard_map/ppermute | solution.py:47
  405.6 36.6 %collective-permute-start.11 = (bf16[64,3584]{1,0:T(8,128)(2,1)S(1)}, bf16[64,3584]{1,0:T(8,128)(2,1)S(1)}, u32[]{:S(2)}, u32[]{:S(2)}) collective-permute-start(bf16[64,3584]{1,0:T(8,128)(2,1)S(1)} %get-tuple-element.9), channel_id=1, source_target_pairs={{0,8},{2,10},{4,12},{6,14},{8,16},{10,18},{12,20},{14,22},{16,24},... | collective-permute-start | bytes 1376264 | tf_op jit(solution)/shard_map/ppermute | solution.py:47
  460.1 8.9 %collective-permute-done.11 = bf16[64,3584]{1,0:T(8,128)(2,1)S(1)} collective-permute-done((bf16[64,3584]{1,0:T(8,128)(2,1)S(1)}, bf16[64,3584]{1,0:T(8,128)(2,1)S(1)}, u32[]{:S(2)}, u32[]{:S(2)}) %collective-permute-start.11) | collective-permute-done | bytes 458784 | tf_op jit(solution)/shard_map/ppermute | solution.py:47
  474.9 10.3 %collective-permute-done.14 = bf16[64,3584]{1,0:T(8,128)(2,1)S(1)} collective-permute-done((bf16[64,3584]{1,0:T(8,128)(2,1)S(1)}, bf16[64,3584]{1,0:T(8,128)(2,1)S(1)}, u32[]{:S(2)}, u32[]{:S(2)}) %collective-permute-start.14) | collective-permute-done | bytes 458784 | tf_op jit(solution)/shard_map/ppermute | solution.py:47
  487.8 12.5 %fusion = bf16[1024,3584]{1,0:T(8,128)(2,1)} fusion(s32[]{:T(128)S(6)} %select_n.31, bf16[1024,3584]{1,0:T(8,128)(2,1)} %slice_dynamic-update-slice_fusion), kind=kLoop, calls=%fused_computation.7 | loop fusion | flops 14680064 | bytes 14680068 | tf_op jit(solution)/shard_map/jit(_roll_dynamic)/concatenate | solution.py:50
  500.3 12.3 %gather_fusion = bf16[512,3584]{1,0:T(8,128)(2,1)} fusion(bf16[1024,3584]{1,0:T(8,128)(2,1)} %fusion, s32[1024]{0:T(1024)S(1)} %pad_clamp_fusion), kind=kCustom, calls=%fused_computation | custom fusion | bytes 7342080 | tf_op jit(solution)/shard_map/gather | solution.py:52
  512.6 5.8 %fusion.2 = bf16[64,3584]{1,0:T(8,128)(2,1)} fusion(bf16[512,3584]{1,0:T(8,128)(2,1)} %gather_fusion, f32[64,8]{1,0:T(8,128)S(1)} %copy.21), kind=kLoop, calls=%fused_computation.10 | loop fusion | flops 5275648 | bytes 4130816 | tf_op jit(solution)/shard_map/reduce_sum | solution.py:53
  (69 shorter events, 55.0 us)
Async XLA Ops:
  6.5 3.6 copy-start
  15.3 165.5 %all-to-all-start = ((bf16[16,64,3584]{2,1,0:T(8,128)(2,1)}), bf16[16,64,3584]{2,1,0:T(8,128)(2,1)}, u32[]{:S(2)}, u32[]{:S(2)}) async-start(bf16[16,64,3584]{2,1,0:T(8,128)(2,1)} %bitcast.53), calls=%async_computation | async-start | bytes 14680064 | tf_op jit(solution)/shard_map/all_to_all | solution.py:27
  22.5 204.7 %reduce-scatter.2.cloned.1.call-start = ((), (), s32[]{:S(2)}) async-start(), calls=%async_computation.2 | async-start | bytes 12582912 | tf_op jit(solution)/shard_map/reduce_scatter | solution.py:32
  202.4 28.9 %copy-start.2 = (f32[64,8]{0,1:T(8,128)S(1)}, f32[64,8]{0,1:T(8,128)}, u32[]{:S(2)}) copy-start(f32[64,8]{0,1:T(8,128)} %param.10) | copy-start | bytes 6148
  202.4 40.6 %all-gather.2.cloned.1.call-start = ((), (), s32[]{:S(2)}) async-start(), calls=%async_computation.3 | async-start | bytes 3145728 | tf_op jit(solution)/shard_map/all_gather | solution.py:35
  273.1 19.4 %collective-permute-start = (bf16[64,3584]{1,0:T(8,128)(2,1)}, bf16[64,3584]{1,0:T(8,128)(2,1)S(1)}, u32[]{:S(2)}, u32[]{:S(2)}) collective-permute-start(bf16[64,3584]{1,0:T(8,128)(2,1)} %get-tuple-element.20), channel_id=1, source_target_pairs={{0,30},{2,0},{4,2},{6,4},{8,6},{10,8},{12,10},{14,12},{16,14},{18,... | collective-permute-start | bytes 1376264 | tf_op jit(solution)/shard_map/ppermute | solution.py:47
  275.5 32.8 %collective-permute-start.1 = (bf16[64,3584]{1,0:T(8,128)(2,1)}, bf16[64,3584]{1,0:T(8,128)(2,1)S(1)}, u32[]{:S(2)}, u32[]{:S(2)}) collective-permute-start(bf16[64,3584]{1,0:T(8,128)(2,1)} %get-tuple-element.19), channel_id=1, source_target_pairs={{0,28},{2,30},{4,0},{6,2},{8,4},{10,6},{12,8},{14,10},{16,12},{18,... | collective-permute-start | bytes 1376264 | tf_op jit(solution)/shard_map/ppermute | solution.py:47
  276.0 42.2 %collective-permute-start.2 = (bf16[64,3584]{1,0:T(8,128)(2,1)}, bf16[64,3584]{1,0:T(8,128)(2,1)S(1)}, u32[]{:S(2)}, u32[]{:S(2)}) collective-permute-start(bf16[64,3584]{1,0:T(8,128)(2,1)} %get-tuple-element.18), channel_id=1, source_target_pairs={{0,26},{2,28},{4,30},{6,0},{8,2},{10,4},{12,6},{14,8},{16,10},{18,... | collective-permute-start | bytes 1376264 | tf_op jit(solution)/shard_map/ppermute | solution.py:47
  279.5 50.7 %collective-permute-start.3 = (bf16[64,3584]{1,0:T(8,128)(2,1)}, bf16[64,3584]{1,0:T(8,128)(2,1)S(1)}, u32[]{:S(2)}, u32[]{:S(2)}) collective-permute-start(bf16[64,3584]{1,0:T(8,128)(2,1)} %get-tuple-element.17), channel_id=1, source_target_pairs={{0,24},{2,26},{4,28},{6,30},{8,0},{10,2},{12,4},{14,6},{16,8},{18,... | collective-permute-start | bytes 1376264 | tf_op jit(solution)/shard_map/ppermute | solution.py:47
  280.0 78.9 %collective-permute-start.4 = (bf16[64,3584]{1,0:T(8,128)(2,1)}, bf16[64,3584]{1,0:T(8,128)(2,1)S(1)}, u32[]{:S(2)}, u32[]{:S(2)}) collective-permute-start(bf16[64,3584]{1,0:T(8,128)(2,1)} %get-tuple-element.16), channel_id=1, source_target_pairs={{0,22},{2,24},{4,26},{6,28},{8,30},{10,0},{12,2},{14,4},{16,6},{18... | collective-permute-start | bytes 1376264 | tf_op jit(solution)/shard_map/ppermute | solution.py:47
  292.5 102.4 %collective-permute-start.5 = (bf16[64,3584]{1,0:T(8,128)(2,1)}, bf16[64,3584]{1,0:T(8,128)(2,1)S(1)}, u32[]{:S(2)}, u32[]{:S(2)}) collective-permute-start(bf16[64,3584]{1,0:T(8,128)(2,1)} %get-tuple-element.15), channel_id=1, source_target_pairs={{0,20},{2,22},{4,24},{6,26},{8,28},{10,30},{12,0},{14,2},{16,4},{1... | collective-permute-start | bytes 1376264 | tf_op jit(solution)/shard_map/ppermute | solution.py:47
  308.3 97.3 %collective-permute-start.6 = (bf16[64,3584]{1,0:T(8,128)(2,1)}, bf16[64,3584]{1,0:T(8,128)(2,1)S(1)}, u32[]{:S(2)}, u32[]{:S(2)}) collective-permute-start(bf16[64,3584]{1,0:T(8,128)(2,1)} %get-tuple-element.14), channel_id=1, source_target_pairs={{0,18},{2,20},{4,22},{6,24},{8,26},{10,28},{12,30},{14,0},{16,2},{... | collective-permute-start | bytes 1376264 | tf_op jit(solution)/shard_map/ppermute | solution.py:47
  318.1 124.9 %collective-permute-start.7 = (bf16[64,3584]{1,0:T(8,128)(2,1)}, bf16[64,3584]{1,0:T(8,128)(2,1)S(1)}, u32[]{:S(2)}, u32[]{:S(2)}) collective-permute-start(bf16[64,3584]{1,0:T(8,128)(2,1)} %get-tuple-element.13), channel_id=1, source_target_pairs={{0,16},{2,18},{4,20},{6,22},{8,24},{10,26},{12,28},{14,30},{16,0},... | collective-permute-start | bytes 1376264 | tf_op jit(solution)/shard_map/ppermute | solution.py:47
  330.1 113.7 %collective-permute-start.8 = (bf16[64,3584]{1,0:T(8,128)(2,1)}, bf16[64,3584]{1,0:T(8,128)(2,1)S(1)}, u32[]{:S(2)}, u32[]{:S(2)}) collective-permute-start(bf16[64,3584]{1,0:T(8,128)(2,1)} %get-tuple-element.12), channel_id=1, source_target_pairs={{0,14},{2,16},{4,18},{6,20},{8,22},{10,24},{12,26},{14,28},{16,30}... | collective-permute-start | bytes 1376264 | tf_op jit(solution)/shard_map/ppermute | solution.py:47
  358.9 90.6 %collective-permute-start.9 = (bf16[64,3584]{1,0:T(8,128)(2,1)}, bf16[64,3584]{1,0:T(8,128)(2,1)S(1)}, u32[]{:S(2)}, u32[]{:S(2)}) collective-permute-start(bf16[64,3584]{1,0:T(8,128)(2,1)} %get-tuple-element.11), channel_id=1, source_target_pairs={{0,12},{2,14},{4,16},{6,18},{8,20},{10,22},{12,24},{14,26},{16,28}... | collective-permute-start | bytes 1376264 | tf_op jit(solution)/shard_map/ppermute | solution.py:47
  394.9 64.4 %collective-permute-start.10 = (bf16[64,3584]{1,0:T(8,128)(2,1)S(1)}, bf16[64,3584]{1,0:T(8,128)(2,1)S(1)}, u32[]{:S(2)}, u32[]{:S(2)}) collective-permute-start(bf16[64,3584]{1,0:T(8,128)(2,1)S(1)} %get-tuple-element.10), channel_id=1, source_target_pairs={{0,10},{2,12},{4,14},{6,16},{8,18},{10,20},{12,22},{14,24},{16,26}... | collective-permute-start | bytes 1376264 | tf_op jit(solution)/shard_map/ppermute | solution.py:47
  405.6 63.4 %collective-permute-start.11 = (bf16[64,3584]{1,0:T(8,128)(2,1)S(1)}, bf16[64,3584]{1,0:T(8,128)(2,1)S(1)}, u32[]{:S(2)}, u32[]{:S(2)}) collective-permute-start(bf16[64,3584]{1,0:T(8,128)(2,1)S(1)} %get-tuple-element.9), channel_id=1, source_target_pairs={{0,8},{2,10},{4,12},{6,14},{8,16},{10,18},{12,20},{14,22},{16,24},... | collective-permute-start | bytes 1376264 | tf_op jit(solution)/shard_map/ppermute | solution.py:47
  443.0 26.8 %collective-permute-start.12 = (bf16[64,3584]{1,0:T(8,128)(2,1)S(1)}, bf16[64,3584]{1,0:T(8,128)(2,1)S(1)}, u32[]{:S(2)}, u32[]{:S(2)}) collective-permute-start(bf16[64,3584]{1,0:T(8,128)(2,1)S(1)} %get-tuple-element.8), channel_id=1, source_target_pairs={{0,6},{2,8},{4,10},{6,12},{8,14},{10,16},{12,18},{14,20},{16,22},{... | collective-permute-start | bytes 1376264 | tf_op jit(solution)/shard_map/ppermute | solution.py:47
  443.9 30.2 %collective-permute-start.13 = (bf16[64,3584]{1,0:T(8,128)(2,1)S(1)}, bf16[64,3584]{1,0:T(8,128)(2,1)S(1)}, u32[]{:S(2)}, u32[]{:S(2)}) collective-permute-start(bf16[64,3584]{1,0:T(8,128)(2,1)S(1)} %get-tuple-element.7), channel_id=1, source_target_pairs={{0,4},{2,6},{4,8},{6,10},{8,12},{10,14},{12,16},{14,18},{16,20},{1... | collective-permute-start | bytes 1376264 | tf_op jit(solution)/shard_map/ppermute | solution.py:47
  449.5 35.7 %collective-permute-start.14 = (bf16[64,3584]{1,0:T(8,128)(2,1)S(1)}, bf16[64,3584]{1,0:T(8,128)(2,1)S(1)}, u32[]{:S(2)}, u32[]{:S(2)}) collective-permute-start(bf16[64,3584]{1,0:T(8,128)(2,1)S(1)} %get-tuple-element.6), channel_id=1, source_target_pairs={{0,2},{2,4},{4,6},{6,8},{8,10},{10,12},{12,14},{14,16},{16,18},{18... | collective-permute-start | bytes 1376264 | tf_op jit(solution)/shard_map/ppermute | solution.py:47
  500.3 18.1 %copy-start.1 = (bf16[64,3584]{1,0:T(8,128)(2,1)S(1)}, bf16[64,3584]{1,0:T(8,128)(2,1)}, u32[]{:S(2)}) copy-start(bf16[64,3584]{1,0:T(8,128)(2,1)} %param.8) | copy-start | bytes 1376260
Sparse Core Ops, SparseCore 0:
  202.5 24.6 reduce-scatter.1
  231.1 11.7 all-gather.1
